TPU v7x, 256 devices: a whole 4x4x8 slice. The times are simulated.
256 devices in a mesh: dp: 4 (over x), seq: 8 (over z_lo, y), tensor: 8 (over z_hi, core).
Axes of the slice: x: 4, y: 4, z: 8 (z_hi: 4, z_lo: 2; z = z_hi * 2 + z_lo), core: 2. Of those that a mesh axis runs over, the one named last changes fastest.
Arguments:
- hidden: bfloat16 [4096, 28672], P(('dp', 'seq'), 'tensor'), may hold values from -6 to 6
- weight: bfloat16 [28672, 4096], P('tensor', 'seq'), may hold values from -0.03125 to 0.03125
- out_grad: bfloat16 [4096, 4096], P(('dp', 'tensor'), 'seq'), may hold values from -6 to 6
Outputs:
- output: bfloat16 [4096, 4096], P(('dp', 'tensor'), 'seq')
- grad_hidden: bfloat16 [4096, 28672], P(('dp', 'seq'), 'tensor')
- grad_weight: bfloat16 [28672, 4096], P('tensor', 'seq')
All inputs are finite; a program needn't handle non-finite values.
Results may differ from a plain program's by a relative error of at most 0.017.
Values may be sent and summed in bfloat16 or wider, within the bound.
A program may use at most 128 MiB of HBM per device.

v0:
```python
import jax
import jax.numpy as jnp
from jax import lax
from jax.sharding import PartitionSpec as P

HB = 512


def partner_2(shard, axis, distance):
    return lax.ppermute(shard, axis, [(i, i ^ 1 << distance) for i in range(lax.axis_size(axis))])


def walsh_table(table_order):
    matrix = jnp.ones((1, 1), jnp.float32)
    while matrix.shape[0] < table_order:
        matrix = jnp.concatenate(
            [jnp.concatenate([matrix, matrix], 1), jnp.concatenate([matrix, -matrix], 1)], 0
        )
    return matrix


def local_blocks(values, inner_table):
    row_count, feature_count = values.shape
    block_size = inner_table.shape[0]
    shaped = values.reshape(row_count, feature_count // block_size, block_size)
    if values.dtype == jnp.bfloat16:
        mixed_rows = jnp.einsum(
            "rbk,kl->rbl",
            shaped,
            inner_table.astype(jnp.bfloat16),
            preferred_element_type=jnp.float32,
        )
    else:
        mixed_rows = jnp.einsum("rbk,kl->rbl", shaped, inner_table, precision=lax.Precision.HIGHEST)
    return mixed_rows.reshape(row_count, feature_count)


def butterfly(values):
    axis_count = lax.axis_size("tensor")
    device_index = lax.axis_index("tensor")
    for bit_index in range(axis_count.bit_length() - 1):
        partner = partner_2(values.astype(jnp.bfloat16), "tensor", bit_index).astype(values.dtype)
        upper_half = device_index // (1 << bit_index) % 2 == 1
        values = jnp.where(upper_half, partner - values, values + partner)
    return values


def rotate(values, inner_table, norm_scale):
    return (butterfly(local_blocks(values, inner_table)) * norm_scale).astype(jnp.bfloat16)


def body(hidden, weight, out_grad):
    inner_table = walsh_table(HB)
    norm_scale = 1.0 / float(lax.axis_size("tensor") * HB) ** 0.5
    rotated = rotate(hidden, inner_table, norm_scale)
    gathered = lax.all_gather(rotated, "seq", axis=0, tiled=True)
    partial_sums = jnp.dot(gathered, weight, preferred_element_type=jnp.float32)
    output = lax.psum_scatter(
        partial_sums.astype(jnp.bfloat16), "tensor", scatter_dimension=0, tiled=True
    )
    grads_all = lax.all_gather(out_grad, "tensor", axis=0, tiled=True)
    token_total = hidden.shape[0] * lax.axis_size("seq") * lax.axis_size("dp")
    grad_term = lax.dot_general(
        gathered, grads_all, (((0,), (0,)), ((), ())), preferred_element_type=jnp.float32
    )
    grad_weight = lax.psum(
        (grad_term * (1.0 / float(token_total) ** 0.5)).astype(jnp.bfloat16), "dp"
    )
    rotated_grad = lax.psum_scatter(
        lax.dot_general(
            grads_all, weight, (((1,), (1,)), ((), ())), preferred_element_type=jnp.float32
        ).astype(jnp.bfloat16),
        "seq",
        scatter_dimension=0,
        tiled=True,
    ).astype(jnp.float32)
    grad_hidden = rotate(rotated_grad, inner_table, norm_scale)
    return (output, grad_hidden, grad_weight)


def solution(mesh):
    in_specs = (P(("dp", "seq"), "tensor"), P("tensor", "seq"), P(("dp", "tensor"), "seq"))
    out_specs = (P(("dp", "tensor"), "seq"), P(("dp", "seq"), "tensor"), P("tensor", "seq"))
    return jax.shard_map(body, mesh=mesh, in_specs=in_specs, out_specs=out_specs, check_vma=False)
```

profile of v0, /device:TPU:1, one launch (start us, length us, event | category | flops | bytes accessed | tf_op | source)
XLA Modules:
  0.0 447.1 jit_solution(14021014759159372248)
XLA Ops:
  7.9 36.3 %all-gather.5.cloned.1.call-done = bf16[1024,512]{1,0:T(8,128)(2,1)} async-done(((bf16[128,512]{1,0:T(8,128)(2,1)}), bf16[1024,512]{1,0:T(8,128)(2,1)}) %all-gather.5.cloned.1.call-update) | async-done | bytes 1048592 | tf_op jit(solution)/shard_map/all_gather | solution.py:61
  44.2 9.3 %convolution_convert_fusion = bf16[1024,3584]{1,0:T(8,128)(2,1)} fusion(bf16[1024,512]{1,0:T(8,128)(2,1)} %all-gather.5.cloned.1.call-done, bf16[3584,512]{1,0:T(8,128)(2,1)} %param.4), kind=kOutput, calls=%fused_computation | convolution fusion | flops 3761766400 | bytes 12058624 | tf_op jit(solution)/shard_map/dot_general | solution.py:70
  57.4 2.4 collective-permute-done
  61.0 1.6 collective-permute-start.1
  62.5 41.3 %collective-permute-done.1 = bf16[128,3584]{0,1:T(8,128)(2,1)} collective-permute-done((bf16[128,3584]{0,1:T(8,128)(2,1)}, bf16[128,3584]{0,1:T(8,128)(2,1)}, u32[]{:S(2)}, u32[]{:S(2)}) %collective-permute-start.1) | collective-permute-done | bytes 917536 | tf_op jit(solution)/shard_map/ppermute | solution.py:10
  103.8 2.6 fusion.11
  106.5 2.7 collective-permute-start.2
  109.2 62.5 %collective-permute-done.2 = bf16[128,3584]{0,1:T(8,128)(2,1)} collective-permute-done((bf16[128,3584]{0,1:T(8,128)(2,1)}, bf16[128,3584]{0,1:T(8,128)(2,1)}, u32[]{:S(2)}, u32[]{:S(2)}) %collective-permute-start.2) | collective-permute-done | bytes 917536 | tf_op jit(solution)/shard_map/ppermute | solution.py:10
  171.7 3.2 fusion.4
  175.0 20.5 %reduce-scatter.5.cloned.1.call-done = bf16[128,3584]{1,0:T(8,128)(2,1)} async-done(((bf16[1024,3584]{1,0:T(8,128)(2,1)}), bf16[128,3584]{1,0:T(8,128)(2,1)}) %reduce-scatter.5.cloned.1.call-update) | async-done | bytes 917520 | tf_op jit(solution)/shard_map/reduce_scatter | solution.py:69
  195.5 1.5 copy.13
  197.0 3.1 fusion.15
  201.5 79.5 %all-gather.3.cloned.1.call-done = bf16[1024,3584]{0,1:T(8,128)(2,1)} async-done(((bf16[128,3584]{0,1:T(8,128)(2,1)}), bf16[1024,3584]{0,1:T(8,128)(2,1)}) %all-gather.3.cloned.1.call-update) | async-done | bytes 7340048 | tf_op jit(solution)/shard_map/all_gather | solution.py:56
  281.0 9.1 %convolution_convert_fusion.1 = bf16[1024,512]{1,0:T(8,128)(2,1)} fusion(bf16[1024,3584]{0,1:T(8,128)(2,1)} %all-gather.3.cloned.1.call-done, bf16[3584,512]{1,0:T(8,128)(2,1)} %param.4), kind=kOutput, calls=%fused_computation.26 | convolution fusion | flops 3758620672 | bytes 12058624 | tf_op jit(solution)/shard_map/dot_general | solution.py:57
  291.4 2.3 collective-permute-start.4
  293.7 8.5 %multiply_convert_fusion = bf16[3584,512]{1,0:T(8,128)(2,1)} fusion(bf16[1024,3584]{0,1:T(8,128)(2,1)} %all-gather.3.cloned.1.call-done, bf16[1024,512]{1,0:T(8,128)(2,1)S(1)} %copy-done.2), kind=kOutput, calls=%fused_computation.1 | convolution fusion | flops 3761766400 | bytes 12058624 | tf_op jit(solution)/shard_map/dot_general | solution.py:63
  302.2 41.2 %collective-permute-done.4 = bf16[128,3584]{0,1:T(8,128)(2,1)} collective-permute-done((bf16[128,3584]{0,1:T(8,128)(2,1)}, bf16[128,3584]{0,1:T(8,128)(2,1)}, u32[]{:S(2)}, u32[]{:S(2)}) %collective-permute-start.4) | collective-permute-done | bytes 917536 | tf_op jit(solution)/shard_map/ppermute | solution.py:10
  343.4 1.7 fusion.10
  345.1 6.5 %collective-permute-start.5 = (bf16[128,3584]{0,1:T(8,128)(2,1)S(1)}, bf16[128,3584]{0,1:T(8,128)(2,1)S(1)}, u32[]{:S(2)}, u32[]{:S(2)}) collective-permute-start(bf16[128,3584]{0,1:T(8,128)(2,1)S(1)} %fusion.10), channel_id=1, source_target_pairs={{0,4},{1,5},{2,6},{3,7},{4,0},{5,1},{6,2},{7,3},{8,12},{9,13},{10,... | collective-permute-start | bytes 2752520 | tf_op jit(solution)/shard_map/ppermute | solution.py:10
  351.6 40.0 %collective-permute-done.5 = bf16[128,3584]{0,1:T(8,128)(2,1)S(1)} collective-permute-done((bf16[128,3584]{0,1:T(8,128)(2,1)S(1)}, bf16[128,3584]{0,1:T(8,128)(2,1)S(1)}, u32[]{:S(2)}, u32[]{:S(2)}) %collective-permute-start.5) | collective-permute-done | bytes 917536 | tf_op jit(solution)/shard_map/ppermute | solution.py:10
  391.6 3.0 fusion.9
  394.6 2.2 copy.16
  396.8 39.6 %all-reduce.2.cloned.1.call-done = bf16[3584,512]{1,0:T(8,128)(2,1)} async-done(((bf16[3584,512]{1,0:T(8,128)(2,1)}), bf16[3584,512]{1,0:T(8,128)(2,1)}) %all-reduce.2.cloned.1.call-update) | async-done | bytes 3670032 | tf_op jit(solution)/shard_map/psum | solution.py:66
  436.4 4.1 copy.21
  (26 shorter events, 8.5 us)
Async XLA Ops:
  7.2 37.1 %all-gather.5.cloned.1.call-start = ((), (), s32[]{:S(2)}) async-start(), calls=%async_computation.4 | async-start | bytes 1179648 | tf_op jit(solution)/shard_map/all_gather | solution.py:61
  7.9 187.6 %reduce-scatter.5.cloned.1.call-start = ((), (), s32[]{:S(2)}) async-start(), calls=%async_computation.5 | async-start | bytes 8257536 | tf_op jit(solution)/shard_map/reduce_scatter | solution.py:69
  53.5 1.2 copy-start
  53.6 1.8 copy-start.1
  53.6 227.5 %all-gather.3.cloned.1.call-start = ((), (), s32[]{:S(2)}) async-start(), calls=%async_computation.2 | async-start | bytes 8257536 | tf_op jit(solution)/shard_map/all_gather | solution.py:56
  57.1 2.7 collective-permute-start
  61.0 42.9 %collective-permute-start.1 = (bf16[128,3584]{0,1:T(8,128)(2,1)}, bf16[128,3584]{0,1:T(8,128)(2,1)}, u32[]{:S(2)}, u32[]{:S(2)}) collective-permute-start(bf16[128,3584]{0,1:T(8,128)(2,1)} %fusion.13), channel_id=1, source_target_pairs={{0,2},{1,3},{2,0},{3,1},{4,6},{5,7},{6,4},{7,5},{8,10},{9,11},{10,... | collective-permute-start | bytes 2752520 | tf_op jit(solution)/shard_map/ppermute | solution.py:10
  106.5 65.2 %collective-permute-start.2 = (bf16[128,3584]{0,1:T(8,128)(2,1)}, bf16[128,3584]{0,1:T(8,128)(2,1)}, u32[]{:S(2)}, u32[]{:S(2)}) collective-permute-start(bf16[128,3584]{0,1:T(8,128)(2,1)} %fusion.11), channel_id=1, source_target_pairs={{0,4},{1,5},{2,6},{3,7},{4,0},{5,1},{6,2},{7,3},{8,12},{9,13},{10,... | collective-permute-start | bytes 2752520 | tf_op jit(solution)/shard_map/ppermute | solution.py:10
  175.0 221.8 %reduce-scatter.3.cloned.1.call-start = ((), (), s32[]{:S(2)}) async-start(), calls=%async_computation.3 | async-start | bytes 1179648 | tf_op jit(solution)/shard_map/reduce_scatter | solution.py:58
  201.1 89.1 %collective-permute-start.3 = (bf16[128,3584]{0,1:T(8,128)(2,1)}, bf16[128,3584]{0,1:T(8,128)(2,1)S(1)}, u32[]{:S(2)}, u32[]{:S(2)}) collective-permute-start(bf16[128,3584]{0,1:T(8,128)(2,1)} %bitcast_convert_fusion), channel_id=1, source_target_pairs={{0,1},{1,0},{2,3},{3,2},{4,5},{5,4},{6,7},{7,6},{8,9},{9,8},{10,11... | collective-permute-start | bytes 2752520 | tf_op jit(solution)/shard_map/ppermute | solution.py:10
  290.1 146.3 %all-reduce.2.cloned.1.call-start = ((), (), s32[]{:S(2)}) async-start(), calls=%async_computation.6 | async-start | bytes 7340032 | tf_op jit(solution)/shard_map/psum | solution.py:66
  290.2 3.5 copy-start.2
  291.4 52.0 %collective-permute-start.4 = (bf16[128,3584]{0,1:T(8,128)(2,1)}, bf16[128,3584]{0,1:T(8,128)(2,1)}, u32[]{:S(2)}, u32[]{:S(2)}) collective-permute-start(bf16[128,3584]{0,1:T(8,128)(2,1)} %fusion.12), channel_id=1, source_target_pairs={{0,2},{1,3},{2,0},{3,1},{4,6},{5,7},{6,4},{7,5},{8,10},{9,11},{10,... | collective-permute-start | bytes 2752520 | tf_op jit(solution)/shard_map/ppermute | solution.py:10
  345.1 46.4 %collective-permute-start.5 = (bf16[128,3584]{0,1:T(8,128)(2,1)S(1)}, bf16[128,3584]{0,1:T(8,128)(2,1)S(1)}, u32[]{:S(2)}, u32[]{:S(2)}) collective-permute-start(bf16[128,3584]{0,1:T(8,128)(2,1)S(1)} %fusion.10), channel_id=1, source_target_pairs={{0,4},{1,5},{2,6},{3,7},{4,0},{5,1},{6,2},{7,3},{8,12},{9,13},{10,... | collective-permute-start | bytes 2752520 | tf_op jit(solution)/shard_map/ppermute | solution.py:10
Sparse Core Ops, SparseCore 0:
  9.8 34.3 all-gather.4
  53.7 141.7 reduce-scatter.4
  197.8 83.2 all-gather.2
  290.3 50.2 reduce-scatter.2
  343.4 93.0 all-reduce.1
where the time goes:
time: 447 us
  waiting for transfers between devices  364 us (81%)
  matrix products  30.6 us (7%)
  other arithmetic  15 us (3%)
  starting transfers between devices  13.9 us (3%)
  between operations  13.8 us (3%)
  local copies, waits for them, and re-layouts  9.58 us (2%)
    ppermute x6, waiting for transfers between devices, partner_2(): lax.ppermute(shard, axis, [(i, i ^ 1 << distance) for i in range(lax.axis...  187 us
    all_gather x1, waiting for transfers between devices, body(): gathered = lax.all_gather(rotated, 'seq', axis=0, tiled=True)  79.5 us
    psum x1, waiting for transfers between devices, body(): lax.psum((grad_term * (1.0 / float(token_total) ** 0.5)).astype(jnp.bfloa...  39.6 us
    all_gather x1, waiting for transfers between devices, body(): grads_all = lax.all_gather(out_grad, 'tensor', axis=0, tiled=True)  36.3 us
    reduce_scatter x1, waiting for transfers between devices, body(): lax.psum_scatter(lax.dot_general(grads_all, weight, (((1,), (1,)), ((), (...  20.5 us
    ppermute x6, starting transfers between devices, partner_2(): lax.ppermute(shard, axis, [(i, i ^ 1 << distance) for i in range(lax.axis...  13.7 us
    dot_general x1, matrix products, body(): lax.dot_general(grads_all, weight, (((1,), (1,)), ((), ())), preferred_el...  9.3 us
    dot_general x1, matrix products, body(): partial_sums = jnp.dot(gathered, weight, preferred_element_type=jnp.float32)  9.08 us
  transfers between devices with their start and end apart: 11, of which 9 were waited for; matrix products, arithmetic and copies ran while one was open for 9% of the time, Pallas kernels for 0%

commit v1 on v0

--- a/solution.py
+++ b/solution.py
@@ -63,8 +63,9 @@
     grad_term = lax.dot_general(
         gathered, grads_all, (((0,), (0,)), ((), ())), preferred_element_type=jnp.float32
     )
-    grad_weight = lax.psum(
-        (grad_term * (1.0 / float(token_total) ** 0.5)).astype(jnp.bfloat16), "dp"
+    grad_weight = jnp.sum(
+        lax.all_gather((grad_term * (1.0 / float(token_total) ** 0.5)).astype(jnp.bfloat16), "dp"),
+        axis=0,
     )
     rotated_grad = lax.psum_scatter(
         lax.dot_general(

time: 447 us -> 490 us (1.096)
  waiting for transfers between devices: 364 us -> 398 us
  other arithmetic: 15 us -> 24.8 us
    reduce_scatter x1, waiting for transfers between devices: 20.5 us -> 82.5 us  [body(): lax.psum_scatter(lax.dot_general(grads_all, weight, (((1,), (1,)), ((), (...]
    psum x1 -> x0, waiting for transfers between devices: 39.6 us -> none  [body(): lax.psum((grad_term * (1.0 / float(token_total) ** 0.5)).astype(jnp.bfloa...]
    all_gather x0 -> x1, waiting for transfers between devices: none -> 35.7 us  [body(): lax.all_gather((grad_term * (1.0 / float(token_total) ** 0.5)).astype(jnp...]
    reduce_scatter x1, waiting for transfers between devices: 0.01 us -> 31.2 us  [body(): lax.psum_scatter(partial_sums.astype(jnp.bfloat16), 'tensor', scatter_dim...]
    all_gather x1, waiting for transfers between devices: 36.3 us -> 6.73 us  [body(): grads_all = lax.all_gather(out_grad, 'tensor', axis=0, tiled=True)]
    ppermute x6, waiting for transfers between devices: 187 us -> 164 us  [partner_2(): lax.ppermute(shard, axis, [(i, i ^ 1 << distance) for i in range(lax.axis...]
    reduce_sum x0 -> x1, other arithmetic: none -> 10.7 us  [body(): jnp.sum(lax.all_gather((grad_term * (1.0 / float(token_total) ** 0.5)).as...]
  transfers between devices with their start and end apart: 11 -> 11, of which waited for: 9 -> 11; matrix products, arithmetic and copies ran while one was open for 9% -> 11% of each run, Pallas kernels for 0% -> 0%
where the time goes in v1:
time: 490 us; the launch traced here: 488 us
  waiting for transfers between devices  398 us (81%)
  matrix products  29.4 us (6%)
  other arithmetic  24.8 us (5%)
  starting transfers between devices  17 us (3%)
  between operations  13.9 us (3%)
  local copies, waits for them, and re-layouts  5.39 us (1%)
    ppermute x6, waiting for transfers between devices, partner_2(): lax.ppermute(shard, axis, [(i, i ^ 1 << distance) for i in range(lax.axis...  164 us
    reduce_scatter x1, waiting for transfers between devices, body(): lax.psum_scatter(lax.dot_general(grads_all, weight, (((1,), (1,)), ((), (...  82.5 us
    all_gather x1, waiting for transfers between devices, body(): gathered = lax.all_gather(rotated, 'seq', axis=0, tiled=True)  77.5 us
    all_gather x1, waiting for transfers between devices, body(): lax.all_gather((grad_term * (1.0 / float(token_total) ** 0.5)).astype(jnp...  35.7 us
    reduce_scatter x1, waiting for transfers between devices, body(): lax.psum_scatter(partial_sums.astype(jnp.bfloat16), 'tensor', scatter_dim...  31.2 us
    ppermute x6, starting transfers between devices, partner_2(): lax.ppermute(shard, axis, [(i, i ^ 1 << distance) for i in range(lax.axis...  16.6 us
    reduce_sum x1, other arithmetic, body(): jnp.sum(lax.all_gather((grad_term * (1.0 / float(token_total) ** 0.5)).as...  10.7 us
  transfers between devices with their start and end apart: 11, of which 11 were waited for; matrix products, arithmetic and copies ran while one was open for 11% of the time, Pallas kernels for 0%

profile of v1, /device:TPU:1, one launch (start us, length us, event | category | flops | bytes accessed | tf_op | source)
XLA Modules:
  0.0 488.3 jit_solution(17500396318208574208)
XLA Ops:
  10.6 3.2 collective-permute-start
  13.8 2.3 collective-permute-done
  18.6 41.6 %collective-permute-done.1 = bf16[128,3584]{0,1:T(8,128)(2,1)} collective-permute-done((bf16[128,3584]{0,1:T(8,128)(2,1)}, bf16[128,3584]{0,1:T(8,128)(2,1)}, u32[]{:S(2)}, u32[]{:S(2)}) %collective-permute-start.1) | collective-permute-done | bytes 917536 | tf_op jit(solution)/shard_map/ppermute | solution.py:10
  60.2 2.6 fusion.11
  62.8 5.0 %collective-permute-start.2 = (bf16[128,3584]{0,1:T(8,128)(2,1)}, bf16[128,3584]{0,1:T(8,128)(2,1)}, u32[]{:S(2)}, u32[]{:S(2)}) collective-permute-start(bf16[128,3584]{0,1:T(8,128)(2,1)} %fusion.11), channel_id=1, source_target_pairs={{0,4},{1,5},{2,6},{3,7},{4,0},{5,1},{6,2},{7,3},{8,12},{9,13},{10,... | collective-permute-start | bytes 2752520 | tf_op jit(solution)/shard_map/ppermute | solution.py:10
  67.9 44.0 %collective-permute-done.2 = bf16[128,3584]{0,1:T(8,128)(2,1)} collective-permute-done((bf16[128,3584]{0,1:T(8,128)(2,1)}, bf16[128,3584]{0,1:T(8,128)(2,1)}, u32[]{:S(2)}, u32[]{:S(2)}) %collective-permute-start.2) | collective-permute-done | bytes 917536 | tf_op jit(solution)/shard_map/ppermute | solution.py:10
  112.0 3.2 fusion.4
  115.3 6.7 %all-gather.7.cloned.1.call-done = bf16[1024,512]{1,0:T(8,128)(2,1)} async-done(((bf16[128,512]{1,0:T(8,128)(2,1)}), bf16[1024,512]{1,0:T(8,128)(2,1)}) %all-gather.7.cloned.1.call-update) | async-done | bytes 1048592 | tf_op jit(solution)/shard_map/all_gather | solution.py:61
  122.0 9.3 %convolution_convert_fusion = bf16[1024,3584]{1,0:T(8,128)(2,1)} fusion(bf16[1024,512]{1,0:T(8,128)(2,1)} %all-gather.7.cloned.1.call-done, bf16[3584,512]{1,0:T(8,128)(2,1)} %param.4), kind=kOutput, calls=%fused_computation | convolution fusion | flops 3761766400 | bytes 12058624 | tf_op jit(solution)/shard_map/dot_general | solution.py:71
  131.4 77.5 %all-gather.5.cloned.1.call-done = bf16[1024,3584]{0,1:T(8,128)(2,1)} async-done(((bf16[128,3584]{0,1:T(8,128)(2,1)}), bf16[1024,3584]{0,1:T(8,128)(2,1)}) %all-gather.5.cloned.1.call-update) | async-done | bytes 7340048 | tf_op jit(solution)/shard_map/all_gather | solution.py:56
  208.9 8.5 %multiply_convert_fusion = bf16[3584,512]{1,0:T(8,128)(2,1)} fusion(bf16[1024,3584]{0,1:T(8,128)(2,1)} %all-gather.5.cloned.1.call-done, bf16[1024,512]{1,0:T(8,128)(2,1)S(1)} %copy-done.2), kind=kOutput, calls=%fused_computation.1 | convolution fusion | flops 3761766400 | bytes 12058624 | tf_op jit(solution)/shard_map/dot_general | solution.py:63
  217.6 82.5 %reduce-scatter.5.cloned.1.call-done = bf16[128,3584]{1,0:T(8,128)(2,1)} async-done(((bf16[1024,3584]{1,0:T(8,128)(2,1)}), bf16[128,3584]{1,0:T(8,128)(2,1)}) %reduce-scatter.5.cloned.1.call-update) | async-done | bytes 917520 | tf_op jit(solution)/shard_map/reduce_scatter | solution.py:70
  301.6 3.1 fusion.15
  305.6 2.1 collective-permute-done.3
  308.9 2.3 collective-permute-start.4
  311.2 7.9 %convolution_convert_fusion.1 = bf16[1024,512]{1,0:T(8,128)(2,1)} fusion(bf16[1024,3584]{0,1:T(8,128)(2,1)} %all-gather.5.cloned.1.call-done, bf16[3584,512]{1,0:T(8,128)(2,1)S(1)} %copy-done.1), kind=kOutput, calls=%fused_computation.26 | convolution fusion | flops 3758620672 | bytes 12058624 | tf_op jit(solution)/shard_map/dot_general | solution.py:57
  319.1 32.9 %collective-permute-done.4 = bf16[128,3584]{0,1:T(8,128)(2,1)} collective-permute-done((bf16[128,3584]{0,1:T(8,128)(2,1)}, bf16[128,3584]{0,1:T(8,128)(2,1)}, u32[]{:S(2)}, u32[]{:S(2)}) %collective-permute-start.4) | collective-permute-done | bytes 917536 | tf_op jit(solution)/shard_map/ppermute | solution.py:10
  353.7 4.0 collective-permute-start.5
  357.7 41.2 %collective-permute-done.5 = bf16[128,3584]{0,1:T(8,128)(2,1)S(1)} collective-permute-done((bf16[128,3584]{0,1:T(8,128)(2,1)S(1)}, bf16[128,3584]{0,1:T(8,128)(2,1)S(1)}, u32[]{:S(2)}, u32[]{:S(2)}) %collective-permute-start.5) | collective-permute-done | bytes 917536 | tf_op jit(solution)/shard_map/ppermute | solution.py:10
  398.9 3.0 fusion.9
  401.9 2.2 copy.16
  404.1 35.7 %all-gather.9.cloned.1.call-done = bf16[14336,512]{1,0:T(8,128)(2,1)} async-done(((bf16[3584,512]{1,0:T(8,128)(2,1)}), bf16[14336,512]{1,0:T(8,128)(2,1)}) %all-gather.9.cloned.1.call-update) | async-done | bytes 14680080 | tf_op jit(solution)/shard_map/all_gather | solution.py:67
  439.8 10.7 %reduce_sum.12 = bf16[3584,512]{1,0:T(8,128)(2,1)} reduce(bf16[4,3584,512]{2,1,0:T(8,128)(2,1)} %bitcast.35, bf16[]{:T(256)} %constant.80.clone.1), dimensions={0}, to_apply=%region_2.3 | reduce | flops 5505024 | bytes 18350082 | tf_op jit(solution)/shard_map/reduce_sum | solution.py:66
  450.5 31.2 %reduce-scatter.3.cloned.1.call-done = bf16[128,512]{1,0:T(8,128)(2,1)} async-done(((bf16[1024,512]{1,0:T(8,128)(2,1)}), bf16[128,512]{1,0:T(8,128)(2,1)}) %reduce-scatter.3.cloned.1.call-update) | async-done | bytes 131088 | tf_op jit(solution)/shard_map/reduce_scatter | solution.py:58
  (26 shorter events, 11.7 us)
Async XLA Ops:
  7.2 1.7 copy-start
  7.2 114.8 %all-gather.7.cloned.1.call-start = ((), (), s32[]{:S(2)}) async-start(), calls=%async_computation.4 | async-start | bytes 1179648 | tf_op jit(solution)/shard_map/all_gather | solution.py:61
  10.6 5.5 %collective-permute-start = (bf16[128,3584]{0,1:T(8,128)(2,1)}, bf16[128,3584]{0,1:T(8,128)(2,1)S(1)}, u32[]{:S(2)}, u32[]{:S(2)}) collective-permute-start(bf16[128,3584]{0,1:T(8,128)(2,1)} %bitcast_convert_fusion.1), channel_id=1, source_target_pairs={{0,1},{1,0},{2,3},{3,2},{4,5},{5,4},{6,7},{7,6},{8,9},{9,8},{10,11... | collective-permute-start | bytes 2752520 | tf_op jit(solution)/shard_map/ppermute | solution.py:10
  17.3 42.9 %collective-permute-start.1 = (bf16[128,3584]{0,1:T(8,128)(2,1)}, bf16[128,3584]{0,1:T(8,128)(2,1)}, u32[]{:S(2)}, u32[]{:S(2)}) collective-permute-start(bf16[128,3584]{0,1:T(8,128)(2,1)} %fusion.13), channel_id=1, source_target_pairs={{0,2},{1,3},{2,0},{3,1},{4,6},{5,7},{6,4},{7,5},{8,10},{9,11},{10,... | collective-permute-start | bytes 2752520 | tf_op jit(solution)/shard_map/ppermute | solution.py:10
  62.8 49.2 %collective-permute-start.2 = (bf16[128,3584]{0,1:T(8,128)(2,1)}, bf16[128,3584]{0,1:T(8,128)(2,1)}, u32[]{:S(2)}, u32[]{:S(2)}) collective-permute-start(bf16[128,3584]{0,1:T(8,128)(2,1)} %fusion.11), channel_id=1, source_target_pairs={{0,4},{1,5},{2,6},{3,7},{4,0},{5,1},{6,2},{7,3},{8,12},{9,13},{10,... | collective-permute-start | bytes 2752520 | tf_op jit(solution)/shard_map/ppermute | solution.py:10
  67.9 141.0 %all-gather.5.cloned.1.call-start = ((), (), s32[]{:S(2)}) async-start(), calls=%async_computation.2 | async-start | bytes 8257536 | tf_op jit(solution)/shard_map/all_gather | solution.py:56
  115.2 184.9 %reduce-scatter.5.cloned.1.call-start = ((), (), s32[]{:S(2)}) async-start(), calls=%async_computation.5 | async-start | bytes 8257536 | tf_op jit(solution)/shard_map/reduce_scatter | solution.py:70
  131.3 77.5 %copy-start.2 = (bf16[1024,512]{1,0:T(8,128)(2,1)S(1)}, bf16[1024,512]{1,0:T(8,128)(2,1)}, u32[]{:S(2)}) copy-start(bf16[1024,512]{1,0:T(8,128)(2,1)} %all-gather.7.cloned.1.call-done) | copy-start | bytes 3145732
  131.3 308.5 %all-gather.9.cloned.1.call-start = ((), (), s32[]{:S(2)}) async-start(), calls=%async_computation.6 | async-start | bytes 18350080 | tf_op jit(solution)/shard_map/all_gather | solution.py:67
  217.4 264.4 %reduce-scatter.3.cloned.1.call-start = ((), (), s32[]{:S(2)}) async-start(), calls=%async_computation.3 | async-start | bytes 1179648 | tf_op jit(solution)/shard_map/reduce_scatter | solution.py:58
  304.8 6.4 %copy-start.1 = (bf16[3584,512]{1,0:T(8,128)(2,1)S(1)}, bf16[3584,512]{1,0:T(8,128)(2,1)}, u32[]{:S(2)}) copy-start(bf16[3584,512]{1,0:T(8,128)(2,1)} %param.4) | copy-start | bytes 11010052
  304.8 2.9 collective-permute-start.3
  308.9 43.1 %collective-permute-start.4 = (bf16[128,3584]{0,1:T(8,128)(2,1)}, bf16[128,3584]{0,1:T(8,128)(2,1)}, u32[]{:S(2)}, u32[]{:S(2)}) collective-permute-start(bf16[128,3584]{0,1:T(8,128)(2,1)} %fusion.12), channel_id=1, source_target_pairs={{0,2},{1,3},{2,0},{3,1},{4,6},{5,7},{6,4},{7,5},{8,10},{9,11},{10,... | collective-permute-start | bytes 2752520 | tf_op jit(solution)/shard_map/ppermute | solution.py:10
  353.7 45.2 %collective-permute-start.5 = (bf16[128,3584]{0,1:T(8,128)(2,1)S(1)}, bf16[128,3584]{0,1:T(8,128)(2,1)S(1)}, u32[]{:S(2)}, u32[]{:S(2)}) collective-permute-start(bf16[128,3584]{0,1:T(8,128)(2,1)S(1)} %fusion.10), channel_id=1, source_target_pairs={{0,4},{1,5},{2,6},{3,7},{4,0},{5,1},{6,2},{7,3},{8,12},{9,13},{10,... | collective-permute-start | bytes 2752520 | tf_op jit(solution)/shard_map/ppermute | solution.py:10
Sparse Core Ops, SparseCore 0:
  68.0 53.9 all-gather.6
  124.3 84.5 all-gather.4
  211.4 88.6 reduce-scatter.4
  302.3 137.4 all-gather.8
  442.8 38.9 reduce-scatter.2
